TPU v7x, 512 devices: a whole 4x8x8 slice. The times are simulated.
512 devices in a mesh: section: 2 (over core), blk: 32 (over z, y_lo), head: 8 (over y_hi, x).
Axes of the slice: x: 4, y: 8 (y_hi: 2, y_lo: 4; y = y_hi * 4 + y_lo), z: 8, core: 2. Of those that a mesh axis runs over, the one named last changes fastest.
Arguments:
- queries: bfloat16 [2, 8192, 8192], P('section', ('blk', 'head')), may hold values from -96 to 96
- key_vectors: bfloat16 [2, 8192, 1024], P('section', ('blk', 'head')), may hold values from -6 to 6
- value_vectors: bfloat16 [2, 8192, 1024], P('section', ('blk', 'head')), may hold values from -6 to 6
- residual: bfloat16 [8192, 8192], P('blk', 'head'), may hold values from -128 to 128
- pair_order: int32 [32], replicated, may hold values from 0 to 31, as said below
- probe_gain: float32 [2, 8192], P('section', 'head'), may hold values from 0.1 to 1.9
- probe_weight: float32 [2, 8192], P('section', 'head'), may hold values from -0.0625 to 0.0625
Outputs:
- hidden_out: bfloat16 [2, 8192, 8192], P('section', 'blk', 'head')
- rewards: float32 [2, 8192], P('section', 'blk')
Inputs may be any that keep to these rules, and one draw needn't show every extreme that they name: `pair_order`: each value appears once.
All inputs are finite; a program needn't handle non-finite values.
Results may differ from a plain program's by a relative error of at most 0.004.
Values may be sent and summed in bfloat16 or wider, within the bound.
No kernel may reach another device: no remote copies, remote signals or barrier semaphores. Data moves between devices by JAX's collectives and lax.ppermute only.
A program may use at most 64 MiB of HBM per device.

v0:
```python
import jax
import jax.numpy as jnp
from jax import lax
from jax.sharding import PartitionSpec as P

D = 8192
HEADS = 64
KV_HEADS = 8
HEAD_DIM = 128
neg_start = -1e30


def sent_together(arrays, axis, dim, along):
    widths = [a.shape[along] for a in arrays]
    both = jnp.concatenate(arrays, axis=along)
    result = lax.all_gather(both, axis, axis=dim, tiled=True)
    return tuple(jnp.split(result, [sum(widths[:k]) for k in range(1, len(widths))], axis=along))


def passed_along(value, axis, steps):
    count = lax.axis_size(axis)
    initial, last = (max(0, -steps), min(count, count - steps))
    return lax.ppermute(value, axis, [(source, source + steps) for source in range(initial, last)])


def copy_for_each(x, axis):
    copies = jnp.broadcast_to(x, (lax.axis_size(axis), *x.shape))
    return lax.all_to_all(copies, axis, split_axis=0, concat_axis=0, tiled=True)


def of_everyone(x, axis):
    everything = copy_for_each(x, axis)
    return jnp.sum(everything, axis=0)


def together(arrays, axis):
    ends = [0]
    for a in arrays:
        ends.append(ends[-1] + a.size)
    total = of_everyone(jnp.concatenate([a.ravel() for a in arrays]), axis)
    return tuple((total[b:e].reshape(a.shape) for a, b, e in zip(arrays, ends, ends[1:])))


def block_first(pair_order, first_row, span_rows):
    count = pair_order.shape[0]
    shard = first_row // (2 * span_rows)
    second = first_row % (2 * span_rows) // span_rows
    lower = jnp.sum(jnp.where(jnp.arange(count, dtype=jnp.int32) == shard, pair_order, 0))
    which = jnp.where(second == 0, lower, 2 * count - 1 - lower)
    return which * span_rows


def update(state, q_part, q_places, key_block, value_block, key_places, factor):
    maxima, totals, accum = state
    scores = (
        jnp.einsum("tkgd,skd->tkgs", q_part, key_block, preferred_element_type=jnp.float32) * factor
    )
    seen = (key_places[None, :] <= q_places[:, None])[:, None, None, :]
    scores = jnp.where(seen, scores, -jnp.inf)
    new_max = jnp.maximum(maxima, jnp.max(scores, axis=-1))
    rescale = jnp.exp(maxima - new_max)
    weights = jnp.exp(scores - new_max[..., None])
    totals = totals * rescale + jnp.sum(weights, axis=-1)
    accum = accum * rescale[..., None] + jnp.einsum(
        "tkgs,skd->tkgd",
        weights.astype(jnp.bfloat16),
        value_block,
        preferred_element_type=jnp.float32,
    )
    return (new_max, totals, accum)


def body(queries, key_vectors, value_vectors, residual, pair_order, probe_gain, probe_weight):
    head_count = lax.axis_size("head")
    q_local, k_local, v_local = (
        lax.all_to_all(queries[0], "head", split_axis=1, concat_axis=0, tiled=True),
        lax.all_to_all(key_vectors[0], "head", split_axis=1, concat_axis=0, tiled=True),
        lax.all_to_all(value_vectors[0], "head", split_axis=1, concat_axis=0, tiled=True),
    )
    row_count = q_local.shape[0]
    span_rows = row_count // 2
    kv_local = KV_HEADS // head_count
    group = HEADS // KV_HEADS
    query_heads = q_local.reshape(row_count, kv_local, group, HEAD_DIM)
    blk_count = lax.axis_size("blk")
    blk_index = lax.axis_index("blk")
    lower = jnp.sum(jnp.where(jnp.arange(blk_count, dtype=jnp.int32) == blk_index, pair_order, 0))
    q_firsts = (lower * span_rows, (2 * blk_count - 1 - lower) * span_rows)
    factor = HEAD_DIM ** (-0.5)
    offsets = jnp.arange(span_rows, dtype=jnp.int32)

    def empty_state():
        return (
            jnp.full((span_rows, kv_local, group), neg_start, jnp.float32),
            jnp.zeros((span_rows, kv_local, group), jnp.float32),
            jnp.zeros((span_rows, kv_local, group, HEAD_DIM), jnp.float32),
        )

    initial = (empty_state(), empty_state())
    carry = initial
    key_piece, value_piece = sent_together((k_local, v_local), "blk", 0, 1)
    blocks = key_piece.shape[0] // span_rows
    key_blocks = key_piece.reshape(blocks, span_rows, kv_local, HEAD_DIM)
    value_blocks = value_piece.reshape(blocks, span_rows, kv_local, HEAD_DIM)
    firsts = jnp.arange(blocks, dtype=jnp.int32) * span_rows

    def key_block(state, inputs):
        key_block_now, value_block_now, first_row = inputs
        key_base = block_first(pair_order, first_row, span_rows)
        key_places = key_base + offsets
        results = []
        for which_half in range(2):
            q_part = query_heads[which_half * span_rows : (which_half + 1) * span_rows]
            q_places = q_firsts[which_half] + offsets

            def compute(inner):
                return update(
                    inner, q_part, q_places, key_block_now, value_block_now, key_places, factor
                )

            def keep(inner):
                return inner

            results.append(
                lax.cond(
                    key_base <= q_firsts[which_half] + span_rows - 1,
                    compute,
                    keep,
                    state[which_half],
                )
            )
        return ((results[0], results[1]), None)

    carry, _ = lax.scan(key_block, carry, (key_blocks, value_blocks, firsts))
    pieces = [state[2] / state[1][..., None] for state in carry]
    attended = jnp.concatenate(pieces, axis=0).reshape(row_count, kv_local * group * HEAD_DIM)
    section_index = lax.axis_index("section")
    own_stream = (residual.astype(jnp.float32) + attended).astype(jnp.bfloat16)
    handed = passed_along(own_stream, "section", 1)
    later_stream = (handed.astype(jnp.float32) + attended).astype(jnp.bfloat16)
    stream = jnp.where(section_index == 0, own_stream, later_stream)
    widened = stream.astype(jnp.float32)
    squares = jnp.sum(widened * widened, axis=-1)
    products = jnp.sum(widened * probe_gain[0][None, :] * probe_weight[0][None, :], axis=-1)
    squares, products = together((squares, products), "head")
    reward = products * lax.rsqrt(squares / D + 1e-05)
    return (stream[None], reward[None])


def solution(mesh):
    return jax.shard_map(
        body,
        mesh=mesh,
        in_specs=(
            P("section", ("blk", "head"), None),
            P("section", ("blk", "head"), None),
            P("section", ("blk", "head"), None),
            P("blk", "head"),
            P(),
            P("section", "head"),
            P("section", "head"),
        ),
        out_specs=(P("section", "blk", "head"), P("section", "blk")),
        check_vma=False,
    )
```

profile of v0, /device:TPU:8, one launch (start us, length us, event | category | flops | bytes accessed | tf_op | source)
XLA Modules:
  0.0 690.0 jit_solution(1719765255200378845)
XLA Ops:
  8.7 8.7 %all-to-all-start = ((bf16[32,8,128]{2,0,1:T(8,128)(2,1)}), bf16[32,8,128]{2,0,1:T(8,128)(2,1)S(1)}, u32[]{:S(2)}, u32[]{:S(2)}) async-start(bf16[32,8,128]{2,0,1:T(8,128)(2,1)} %copy.42), calls=%async_computation | async-start | bytes 131072 | tf_op jit(solution)/shard_map/all_to_all | solution.py:77
  18.3 9.3 %all-to-all-done = bf16[32,8,128]{2,0,1:T(8,128)(2,1)S(1)} async-done(((bf16[32,8,128]{2,0,1:T(8,128)(2,1)}), bf16[32,8,128]{2,0,1:T(8,128)(2,1)S(1)}, u32[]{:S(2)}, u32[]{:S(2)}) %all-to-all-start) | async-done | bytes 65568 | tf_op jit(solution)/shard_map/all_to_all | solution.py:77
  27.6 12.7 %all_to_all.60 = bf16[32,8,128]{2,0,1:T(8,128)(2,1)S(1)} all-to-all(bf16[32,8,128]{2,0,1:T(8,128)(2,1)S(1)} %copy.43), channel_id=1, replica_groups=mesh['section'=2,'blk'=32,'head'=8] {'head'}, dimensions={1} | all-to-all | bytes 131072 | tf_op jit(solution)/shard_map/all_to_all | solution.py:78
  40.9 1.3 copy.55
  42.3 1.1 copy.44
  43.4 3.5 all-to-all-start.2
  48.8 18.0 %all-to-all-done.2 = bf16[32,8,1024]{2,0,1:T(8,128)(2,1)S(1)} async-done(((bf16[32,8,1024]{2,0,1:T(8,128)(2,1)}), bf16[32,8,1024]{2,0,1:T(8,128)(2,1)S(1)}, u32[]{:S(2)}, u32[]{:S(2)}) %all-to-all-start.2) | async-done | bytes 524320 | tf_op jit(solution)/shard_map/all_to_all | solution.py:76
  67.0 140.6 %all-gather.2.cloned.1.call-done = bf16[8192,256]{1,0:T(8,128)(2,1)} async-done(((bf16[256,256]{1,0:T(8,128)(2,1)}), bf16[8192,256]{1,0:T(8,128)(2,1)}) %all-gather.2.cloned.1.call-update) | async-done | bytes 4194320 | tf_op jit(solution)/shard_map/all_gather | solution.py:16
  207.6 4.5 fusion.39
  212.2 445.3 %while.25 = (s32[]{:T(128)}, f32[128,1,8]{0,2,1:T(8,128)S(1)}, f32[128,1,8]{0,2,1:T(8,128)S(1)}, f32[128,1,8,128]{3,0,2,1:T(8,128)S(1)}, f32[128,1,8]{0,2,1:T(8,...) while((s32[]{:T(128)}, f32[128,1,8]{0,2,1:T(8,128)S(1)}, ...), condition=%wide.region_11.12_spmd.clone.clone, body=%wide.region_1.11_spmd.clone.clone.sunk | while | flops 136616448 | bytes 6232100 | solution.py:134
  218.2 0.9 conditional.9
  225.1 0.9 conditional.9
  232.1 0.9 conditional.9
  233.0 0.9 conditional.8
  239.9 0.9 conditional.9
  246.9 0.9 conditional.9
  247.8 0.9 conditional.8
  260.8 0.9 conditional.9
  267.7 0.9 conditional.9
  274.6 0.9 conditional.9
  281.6 0.9 conditional.9
  288.5 0.9 conditional.9
  295.5 0.9 conditional.9
  309.4 0.9 conditional.9
  316.3 0.9 conditional.9
  317.2 0.9 conditional.8
  330.2 0.9 conditional.9
  337.1 0.9 conditional.9
  351.0 0.9 conditional.9
  364.9 0.9 conditional.9
  372.8 0.9 conditional.8
  385.7 0.9 conditional.9
  392.7 0.9 conditional.9
  406.6 0.9 conditional.9
  420.4 0.9 conditional.9
  434.3 0.9 conditional.9
  448.2 0.9 conditional.9
  455.2 0.9 conditional.9
  456.1 0.9 conditional.8
  469.1 0.9 conditional.9
  470.0 0.9 conditional.8
  482.9 0.9 conditional.9
  489.9 0.9 conditional.9
  503.8 0.9 conditional.9
  510.7 0.9 conditional.9
  517.7 0.9 conditional.9
  524.6 0.9 conditional.9
  531.5 0.9 conditional.9
  545.4 0.9 conditional.9
  559.3 0.9 conditional.9
  580.1 0.9 conditional.9
  581.1 0.9 conditional.8
  594.0 0.9 conditional.9
  601.0 0.9 conditional.9
  614.9 0.9 conditional.9
  622.8 0.9 conditional.8
  635.7 0.9 conditional.9
  642.6 0.9 conditional.9
  649.6 0.9 conditional.9
  656.5 0.9 conditional.9
  659.2 1.3 collective-permute-start
  660.6 1.5 collective-permute-done
  662.1 1.1 fusion.29
  663.2 19.3 %all_to_all.61 = f32[8,1,512]{2,1,0:T(1,128)S(1)} all-to-all(f32[8,1,512]{2,1,0:T(1,128)S(1)} %broadcast_in_dim.54), channel_id=1, replica_groups=mesh['section'=2,'blk'=32,'head'=8] {'head'}, dimensions={0} | all-to-all | bytes 32768 | tf_op jit(solution)/shard_map/all_to_all | solution.py:28
  (951 shorter events, 205.9 us)
Async XLA Ops:
  8.0 38.9 %copy-start.3 = (s32[32]{0:T(128)S(1)}, s32[32]{0:T(128)}, u32[]{:S(2)}) copy-start(s32[32]{0:T(128)} %param.17) | copy-start | bytes 388
  8.7 18.9 %all-to-all-start = ((bf16[32,8,128]{2,0,1:T(8,128)(2,1)}), bf16[32,8,128]{2,0,1:T(8,128)(2,1)S(1)}, u32[]{:S(2)}, u32[]{:S(2)}) async-start(bf16[32,8,128]{2,0,1:T(8,128)(2,1)} %copy.42), calls=%async_computation | async-start | bytes 131072 | tf_op jit(solution)/shard_map/all_to_all | solution.py:77
  17.3 190.3 %all-gather.2.cloned.1.call-start = ((), (), s32[]{:S(2)}) async-start(), calls=%async_computation.4 | async-start | bytes 4325376 | tf_op jit(solution)/shard_map/all_gather | solution.py:16
  43.4 23.5 %all-to-all-start.2 = ((bf16[32,8,1024]{2,0,1:T(8,128)(2,1)}), bf16[32,8,1024]{2,0,1:T(8,128)(2,1)S(1)}, u32[]{:S(2)}, u32[]{:S(2)}) async-start(bf16[32,8,1024]{2,0,1:T(8,128)(2,1)} %copy.44), calls=%async_computation.2 | async-start | bytes 1048576 | tf_op jit(solution)/shard_map/all_to_all | solution.py:76
  657.9 1.0 copy-start
  657.9 4.1 copy-start.1
  658.0 4.1 copy-start.2
  659.2 2.8 collective-permute-start
Sparse Core Ops, SparseCore 0:
  41.1 166.4 all-gather.1
where the time goes:
time: 698 us; the launch traced here: 690 us
  loops' own time  260 us (37%)
  waiting for transfers between devices  169 us (24%)
  local copies, waits for them, and re-layouts  98.7 us (14%)
  other arithmetic  57.1 us (8%)
  matrix products  43.4 us (6%)
  blocking collectives  32 us (5%)
  between operations  15.5 us (2%)
  starting transfers between devices  13.5 us (2%)
    another operation x1, loops' own time, body(): carry, _ = lax.scan(key_block, carry, (key_blocks, value_blocks, firsts))  255 us
    all_gather x1, waiting for transfers between devices, sent_together(): result = lax.all_gather(both, axis, axis=dim, tiled=True)  141 us
    squeeze x64, local copies, waits for them, and re-layouts, body(): carry, _ = lax.scan(key_block, carry, (key_blocks, value_blocks, firsts))  50.4 us
    reduce_sum x64, other arithmetic, block_first(): jnp.sum(jnp.where(jnp.arange(count, dtype=jnp.int32) == shard, pair_order...  40.4 us
    dynamic_slice x64, local copies, waits for them, and re-layouts, body(): carry, _ = lax.scan(key_block, carry, (key_blocks, value_blocks, firsts))  37.6 us
    dot_general x65, matrix products, update(): jnp.einsum('tkgs,skd->tkgd', weights.astype(jnp.bfloat16), value_block, p...  28 us
    all_to_all x1, blocking collectives, copy_for_each(): return lax.all_to_all(copies, axis, split_axis=0, concat_axis=0, tiled=True)  19.3 us
    all_to_all x1, waiting for transfers between devices, body(): lax.all_to_all(queries[0], 'head', split_axis=1, concat_axis=0, tiled=True)  18 us
  transfers between devices with their start and end apart: 4, of which 4 were waited for; matrix products, arithmetic and copies ran while one was open for 1% of the time, Pallas kernels for 0%

commit v1 on v0

--- a/solution.py
+++ b/solution.py
@@ -72,9 +72,18 @@
 
 def body(queries, key_vectors, value_vectors, residual, pair_order, probe_gain, probe_weight):
     head_count = lax.axis_size("head")
+    detail_the_types = lambda sheet: jnp.concatenate(
+        jax.lax.all_to_all(
+            jnp.stack(jnp.split(sheet, jax.lax.axis_size("head"), axis=1)),
+            axis_name="head",
+            concat_axis=0,
+            split_axis=0,
+        ),
+        axis=0,
+    )
     q_local, k_local, v_local = (
         lax.all_to_all(queries[0], "head", split_axis=1, concat_axis=0, tiled=True),
-        lax.all_to_all(key_vectors[0], "head", split_axis=1, concat_axis=0, tiled=True),
+        detail_the_types(key_vectors[0]),
         lax.all_to_all(value_vectors[0], "head", split_axis=1, concat_axis=0, tiled=True),
     )
     row_count = q_local.shape[0]

time: 698 us -> 707 us (1.013)
  local copies, waits for them, and re-layouts: 98.7 us -> 108 us
    unnamed x13 -> x19, local copies, waits for them, and re-layouts: 3.54 us -> 11.8 us
where the time goes in v1:
time: 707 us; the launch traced here: 699 us
  loops' own time  260 us (37%)
  waiting for transfers between devices  169 us (24%)
  local copies, waits for them, and re-layouts  108 us (15%)
  other arithmetic  57.1 us (8%)
  matrix products  43.3 us (6%)
  blocking collectives  32 us (5%)
  between operations  15.5 us (2%)
  starting transfers between devices  13.5 us (2%)
    another operation x1, loops' own time, body(): carry, _ = lax.scan(key_block, carry, (key_blocks, value_blocks, firsts))  255 us
    all_gather x1, waiting for transfers between devices, sent_together(): result = lax.all_gather(both, axis, axis=dim, tiled=True)  141 us
    squeeze x64, local copies, waits for them, and re-layouts, body(): carry, _ = lax.scan(key_block, carry, (key_blocks, value_blocks, firsts))  50.4 us
    reduce_sum x64, other arithmetic, block_first(): jnp.sum(jnp.where(jnp.arange(count, dtype=jnp.int32) == shard, pair_order...  40.5 us
    dynamic_slice x64, local copies, waits for them, and re-layouts, body(): carry, _ = lax.scan(key_block, carry, (key_blocks, value_blocks, firsts))  37.6 us
    dot_general x65, matrix products, update(): jnp.einsum('tkgs,skd->tkgd', weights.astype(jnp.bfloat16), value_block, p...  28 us
    all_to_all x1, blocking collectives, copy_for_each(): return lax.all_to_all(copies, axis, split_axis=0, concat_axis=0, tiled=True)  19.3 us
    all_to_all x1, waiting for transfers between devices, body(): lax.all_to_all(queries[0], 'head', split_axis=1, concat_axis=0, tiled=True)  18 us
  transfers between devices with their start and end apart: 4, of which 4 were waited for; matrix products, arithmetic and copies ran while one was open for 1% of the time, Pallas kernels for 0%

profile of v1, /device:TPU:8, one launch (start us, length us, event | category | flops | bytes accessed | tf_op | source)
XLA Modules:
  0.0 698.7 jit_solution(5658894409696280835)
XLA Ops:
  7.2 1.3 constant_dynamic-update-slice_fusion.7
  8.5 1.3 constant_dynamic-update-slice_fusion.6
  9.8 1.3 constant_dynamic-update-slice_fusion.5
  11.1 1.3 constant_dynamic-update-slice_fusion.4
  12.4 1.3 constant_dynamic-update-slice_fusion.3
  13.7 1.3 constant_dynamic-update-slice_fusion.2
  15.0 1.3 constant_dynamic-update-slice_fusion.1
  16.3 1.3 constant_dynamic-update-slice_fusion
  17.6 8.7 %all-to-all-start = ((bf16[8,32,128]{2,1,0:T(8,128)(2,1)}), bf16[8,32,128]{2,1,0:T(8,128)(2,1)S(1)}, u32[]{:S(2)}, u32[]{:S(2)}) async-start(bf16[8,32,128]{2,1,0:T(8,128)(2,1)} %constant_dynamic-update-slice_fusion), calls=%async_computation | async-start | bytes 131072 | tf_op jit(solution)/shard_map/all_to_all | solution.py:76
  27.1 9.3 %all-to-all-done = bf16[8,32,128]{2,1,0:T(8,128)(2,1)S(1)} async-done(((bf16[8,32,128]{2,1,0:T(8,128)(2,1)}), bf16[8,32,128]{2,1,0:T(8,128)(2,1)S(1)}, u32[]{:S(2)}, u32[]{:S(2)}) %all-to-all-start) | async-done | bytes 65568 | tf_op jit(solution)/shard_map/all_to_all | solution.py:76
  36.5 12.7 %all_to_all.46 = bf16[32,8,128]{2,0,1:T(8,128)(2,1)S(1)} all-to-all(bf16[32,8,128]{2,0,1:T(8,128)(2,1)S(1)} %copy.38), channel_id=1, replica_groups=mesh['section'=2,'blk'=32,'head'=8] {'head'}, dimensions={1} | all-to-all | bytes 131072 | tf_op jit(solution)/shard_map/all_to_all | solution.py:87
  49.8 1.3 copy.49
  51.2 1.1 copy.39
  52.3 3.5 all-to-all-start.2
  57.7 18.0 %all-to-all-done.2 = bf16[32,8,1024]{2,0,1:T(8,128)(2,1)S(1)} async-done(((bf16[32,8,1024]{2,0,1:T(8,128)(2,1)}), bf16[32,8,1024]{2,0,1:T(8,128)(2,1)S(1)}, u32[]{:S(2)}, u32[]{:S(2)}) %all-to-all-start.2) | async-done | bytes 524320 | tf_op jit(solution)/shard_map/all_to_all | solution.py:85
  75.9 140.6 %all-gather.2.cloned.1.call-done = bf16[8192,256]{1,0:T(8,128)(2,1)} async-done(((bf16[256,256]{1,0:T(8,128)(2,1)}), bf16[8192,256]{1,0:T(8,128)(2,1)}) %all-gather.2.cloned.1.call-update) | async-done | bytes 4194320 | tf_op jit(solution)/shard_map/all_gather | solution.py:16
  216.5 4.5 fusion.39
  221.1 445.1 %while.25 = (s32[]{:T(128)}, f32[128,1,8]{0,2,1:T(8,128)S(1)}, f32[128,1,8]{0,2,1:T(8,128)S(1)}, f32[128,1,8,128]{3,0,2,1:T(8,128)S(1)}, f32[128,1,8]{0,2,1:T(8,...) while((s32[]{:T(128)}, f32[128,1,8]{0,2,1:T(8,128)S(1)}, ...), condition=%wide.region_11.12_spmd.clone.clone, body=%wide.region_1.11_spmd.clone.clone.sunk | while | flops 136616448 | bytes 6232100 | solution.py:143
  234.0 0.9 conditional.9
  240.9 0.9 conditional.9
  241.9 0.9 conditional.8
  248.8 0.9 conditional.9
  255.7 0.9 conditional.9
  256.7 0.9 conditional.8
  269.6 0.9 conditional.9
  276.6 0.9 conditional.9
  283.5 0.9 conditional.9
  290.4 0.9 conditional.9
  297.4 0.9 conditional.9
  304.3 0.9 conditional.9
  311.3 0.9 conditional.9
  318.2 0.9 conditional.9
  325.1 0.9 conditional.9
  326.1 0.9 conditional.8
  339.0 0.9 conditional.9
  346.0 0.9 conditional.9
  352.9 0.9 conditional.9
  359.8 0.9 conditional.9
  366.8 0.9 conditional.9
  373.7 0.9 conditional.9
  380.7 0.9 conditional.9
  381.6 0.9 conditional.8
  394.5 0.9 conditional.9
  401.5 0.9 conditional.9
  408.4 0.9 conditional.9
  415.4 0.9 conditional.9
  422.3 0.9 conditional.9
  429.2 0.9 conditional.9
  436.2 0.9 conditional.9
  464.9 0.9 conditional.8
  477.8 0.9 conditional.9
  478.8 0.9 conditional.8
  491.7 0.9 conditional.9
  498.6 0.9 conditional.9
  589.8 0.9 conditional.8
  602.7 0.9 conditional.9
  609.7 0.9 conditional.9
  631.4 0.9 conditional.8
  644.4 0.9 conditional.9
  651.3 0.9 conditional.9
  667.9 1.3 collective-permute-start
  669.2 1.5 collective-permute-done
  670.7 1.1 fusion.29
  671.9 19.3 %all_to_all.47 = f32[8,1,512]{2,1,0:T(1,128)S(1)} all-to-all(f32[8,1,512]{2,1,0:T(1,128)S(1)} %broadcast_in_dim.54), channel_id=1, replica_groups=mesh['section'=2,'blk'=32,'head'=8] {'head'}, dimensions={0} | all-to-all | bytes 32768 | tf_op jit(solution)/shard_map/all_to_all | solution.py:28
  (957 shorter events, 211.7 us)
Async XLA Ops:
  8.5 47.3 %copy-start.3 = (s32[32]{0:T(128)S(1)}, s32[32]{0:T(128)}, u32[]{:S(2)}) copy-start(s32[32]{0:T(128)} %param.17) | copy-start | bytes 388
  17.6 18.9 %all-to-all-start = ((bf16[8,32,128]{2,1,0:T(8,128)(2,1)}), bf16[8,32,128]{2,1,0:T(8,128)(2,1)S(1)}, u32[]{:S(2)}, u32[]{:S(2)}) async-start(bf16[8,32,128]{2,1,0:T(8,128)(2,1)} %constant_dynamic-update-slice_fusion), calls=%async_computation | async-start | bytes 131072 | tf_op jit(solution)/shard_map/all_to_all | solution.py:76
  26.2 190.3 %all-gather.2.cloned.1.call-start = ((), (), s32[]{:S(2)}) async-start(), calls=%async_computation.4 | async-start | bytes 4325376 | tf_op jit(solution)/shard_map/all_gather | solution.py:16
  52.3 23.5 %all-to-all-start.2 = ((bf16[32,8,1024]{2,0,1:T(8,128)(2,1)}), bf16[32,8,1024]{2,0,1:T(8,128)(2,1)S(1)}, u32[]{:S(2)}, u32[]{:S(2)}) async-start(bf16[32,8,1024]{2,0,1:T(8,128)(2,1)} %copy.39), calls=%async_computation.2 | async-start | bytes 1048576 | tf_op jit(solution)/shard_map/all_to_all | solution.py:85
  666.5 1.0 copy-start
  666.6 4.1 copy-start.1
  666.6 4.1 copy-start.2
  667.9 2.8 collective-permute-start
Sparse Core Ops, SparseCore 0:
  50.0 166.4 all-gather.1
